TPU v7x, 32 devices: a whole 2x2x4 slice. The times are simulated.
32 devices in a mesh: fsdp: 16 (over z, y, core), expert: 2 (over x).
Axes of the slice: x: 2, y: 2, z: 4, core: 2. Of those that a mesh axis runs over, the one named last changes fastest.
Arguments:
- tokens: bfloat16 [8192, 1024], P(('fsdp', 'expert')), may hold values from -6 to 6
- query_weight: bfloat16 [1024, 1024], P(('fsdp', 'expert')), may hold values from -0.1875 to 0.1875
- key_projection: bfloat16 [1024, 512], P(('fsdp', 'expert')), may hold values from -0.1875 to 0.1875
- value_projection: bfloat16 [1024, 512], P(('fsdp', 'expert')), may hold values from -0.1875 to 0.1875
- output_weight: bfloat16 [1024, 1024], P(('fsdp', 'expert')), may hold values from -0.75 to 0.75
- router_weight: bfloat16 [1024, 32], P(('fsdp', 'expert')), may hold values from -0.375 to 0.375
- attn_gain: bfloat16 [1024], P(('fsdp', 'expert')), may hold values from 0.5 to 1.5
- ffn_gain: bfloat16 [1024], P(('fsdp', 'expert')), may hold values from 0.5 to 1.5
- gate_weight: bfloat16 [32, 1024, 512], P('expert', 'fsdp'), may hold values from -0.1875 to 0.1875
- up_weight: bfloat16 [32, 1024, 512], P('expert', 'fsdp'), may hold values from -0.1875 to 0.1875
- down_weight: bfloat16 [32, 512, 1024], P('expert', 'fsdp'), may hold values from -0.75 to 0.75
- lengths: int32 [32, 2, 4], P(('fsdp', 'expert')), may hold values from 1 to 64, 128 in all within a row
- routes: int32 [8192, 8], P(('fsdp', 'expert')), may hold values from 0 to 31, all different within a row; in each aligned block of 128 rows (0 to 127, 128 to 255, ...) at most 40 rows name the same one
- cotangent: bfloat16 [8192, 1024], P(('fsdp', 'expert')), may hold values from -6 to 6
Outputs:
- layer_out: bfloat16 [8192, 1024], P(('fsdp', 'expert'))
- grad_tokens: float32 [8192, 1024], P(('fsdp', 'expert'))
- grad_query: float32 [1024, 1024], P(('fsdp', 'expert'))
- grad_key: float32 [1024, 512], P(('fsdp', 'expert'))
- grad_value: float32 [1024, 512], P(('fsdp', 'expert'))
- grad_output: float32 [1024, 1024], P(('fsdp', 'expert'))
- grad_router: float32 [1024, 32], P(('fsdp', 'expert'))
- grad_attn_gain: float32 [1024], P(('fsdp', 'expert'))
- grad_ffn_gain: float32 [1024], P(('fsdp', 'expert'))
- grad_gate: float32 [32, 1024, 512], P('expert', 'fsdp')
- grad_up: float32 [32, 1024, 512], P('expert', 'fsdp')
- grad_down: float32 [32, 512, 1024], P('expert', 'fsdp')
Inputs may be any that keep to these rules, and one draw needn't show every extreme that they name: Each micro-batch of each device holds 4 sequences whose lengths sum to 128; the longest is exactly 64 tokens in every micro-batch. `routes`: the 8 experts of a row differ; in each aligned block of 128 rows (one micro-batch of one device) no expert is named by more than 40 rows, a bound that some block reaches.
All inputs are finite; a program needn't handle non-finite values.
Results may differ from a plain program's by a relative error of at most 0.015.
The roundings to bfloat16 on the way count: a program that leaves them out, or rounds other values in their place, can miss the bound.
Values may be sent and summed in bfloat16 or wider, within the bound.
No kernel may reach another device: no remote copies, remote signals or barrier semaphores. Data moves between devices by JAX's collectives and lax.ppermute only.
A program may use at most 256 MiB of HBM per device.

v0:
```python
import jax
import jax.numpy as jnp
from jax import lax
from jax.sharding import PartitionSpec as P

MODEL_WIDTH = 1024
QUERY_HEADS = 16
KEY_VALUE_HEADS = 8
HEAD_SIZE = 64
EXPERTS = 32
DEVICE_TOKENS = 128
MB = 2
CAP = 40
ROWS = MB * DEVICE_TOKENS
SLOTS = MB * CAP
Q_COLS = QUERY_HEADS * HEAD_SIZE
KV_COLS = KEY_VALUE_HEADS * HEAD_SIZE
QKV_COLS = Q_COLS + 2 * KV_COLS
SMALL_COLS = 128
EPS = 1e-06
THETA = 10000.0
SCALE = 0.125
HIGH = lax.Precision.HIGHEST
BOTH = ("fsdp", "expert")
F32 = jnp.float32
BF16 = jnp.bfloat16


def mm(spec, a, b):
    return jnp.einsum(spec, a, b, preferred_element_type=F32)


def sequence_layout(seq_lengths, row_number):
    row_index = jnp.arange(row_number, dtype=jnp.int32)
    seq_ends = jnp.cumsum(seq_lengths)
    starts = seq_ends - seq_lengths
    member = (
        (row_index[:, None] >= starts[None, :]) & (row_index[:, None] < seq_ends[None, :])
    ).astype(jnp.int32)
    labels = jnp.arange(seq_lengths.shape[0], dtype=jnp.int32)
    segment = jnp.sum(member * labels[None, :], axis=1)
    offset = jnp.sum(member * starts[None, :], axis=1)
    return (segment, row_index - offset)


def rotary_tables(token_positions):
    half_width = HEAD_SIZE // 2
    frequency = THETA ** (-2.0 * jnp.arange(half_width, dtype=F32) / HEAD_SIZE)
    angles = token_positions.astype(F32)[:, None] * frequency[None, :]
    return (jnp.cos(angles)[:, None, :], jnp.sin(angles)[:, None, :])


def rotary_apply(values, cosine, sine_part):
    half_width = HEAD_SIZE // 2
    first_half = values[..., :half_width]
    second_half = values[..., half_width:]
    return jnp.concatenate(
        [
            first_half * cosine - second_half * sine_part,
            second_half * cosine + first_half * sine_part,
        ],
        axis=-1,
    )


def rms_scale(values):
    return lax.rsqrt(jnp.mean(values * values, axis=1, keepdims=True) + EPS)


def norm_back(grad_normed, gain_vec, plain_part, scale_part):
    grad_gain = jnp.sum(grad_normed * plain_part, axis=0)
    shaped = grad_normed * gain_vec[None, :]
    grad_input = scale_part * (
        shaped - plain_part * jnp.mean(shaped * plain_part, axis=1, keepdims=True)
    )
    return (grad_input, grad_gain)


def fsdp_groups(local_experts):
    size = lax.axis_size("fsdp")
    runs = size // local_experts
    if runs == 1:
        return (None, None)
    inner = [[s * local_experts + j for j in range(local_experts)] for s in range(runs)]
    cross = [[s * local_experts + j for s in range(runs)] for j in range(local_experts)]
    return (inner, cross)


def weight_to_expert(weight, inner, cross):
    part = lax.all_to_all(
        weight, "fsdp", split_axis=0, concat_axis=1, axis_index_groups=inner, tiled=True
    )[0]
    if cross is not None:
        part = lax.all_gather(part, "fsdp", axis=0, axis_index_groups=cross, tiled=True)
    return part


def grad_to_owners(grad, inner, cross):
    if cross is not None:
        grad = lax.psum_scatter(
            grad, "fsdp", scatter_dimension=0, axis_index_groups=cross, tiled=True
        )
    return lax.all_to_all(
        grad.astype(BF16)[None],
        "fsdp",
        split_axis=1,
        concat_axis=0,
        axis_index_groups=inner,
        tiled=True,
    ).astype(F32)


def exchange(rows, local_experts, inner):
    if inner is None:
        return lax.all_to_all(rows, BOTH, split_axis=0, concat_axis=0, tiled=True)
    groups = EXPERTS // local_experts
    shaped = rows.reshape((local_experts, groups) + rows.shape[1:])
    shaped = lax.all_to_all(
        shaped, "fsdp", split_axis=0, concat_axis=0, axis_index_groups=inner, tiled=True
    )
    shaped = lax.all_to_all(shaped, "expert", split_axis=1, concat_axis=1, tiled=True)
    return shaped.reshape(rows.shape)


def sum_to_owners(grad):
    devices = lax.axis_size(BOTH)
    parts = grad.reshape(devices, grad.shape[0] // devices, grad.shape[1])
    parts = lax.all_to_all(parts, BOTH, split_axis=0, concat_axis=0, tiled=True)
    return jnp.sum(parts.astype(F32), axis=0)


def per_device(
    tokens,
    query_weight,
    key_projection,
    value_projection,
    output_weight,
    router_weight,
    attn_gain,
    ffn_gain,
    gate_weight,
    up_weight,
    down_weight,
    lengths,
    routes,
    cotangent,
):
    local_experts = gate_weight.shape[0]
    groups = EXPERTS // local_experts
    inner, cross = fsdp_groups(local_experts)
    heads = QUERY_HEADS // KEY_VALUE_HEADS
    small = jnp.concatenate(
        [
            router_weight,
            attn_gain[:, None],
            ffn_gain[:, None],
            jnp.zeros((router_weight.shape[0], SMALL_COLS - EXPERTS - 2), BF16),
        ],
        axis=1,
    )
    packed = jnp.concatenate(
        [query_weight, key_projection, value_projection, output_weight, small], axis=1
    )
    full = lax.all_gather(packed, BOTH, axis=0, tiled=True)
    qkv_full = full[:, :QKV_COLS]
    o_full = full[:, QKV_COLS : QKV_COLS + MODEL_WIDTH]
    small_full = full[:, QKV_COLS + MODEL_WIDTH :]
    r_full = small_full[:, :EXPERTS]
    gain_one = small_full[:, EXPERTS].astype(F32)
    gain_two = small_full[:, EXPERTS + 1].astype(F32)
    gate_full = weight_to_expert(gate_weight, inner, cross)
    up_full = weight_to_expert(up_weight, inner, cross)
    down_full = weight_to_expert(down_weight, inner, cross)
    plain_in = tokens.astype(F32)
    grad_out = cotangent.astype(F32)
    layouts = [sequence_layout(lengths[0, b], DEVICE_TOKENS) for b in range(MB)]
    segment = jnp.stack([s for s, _ in layouts])
    cosine, sine = rotary_tables(jnp.concatenate([p for _, p in layouts]))
    row_index = jnp.arange(DEVICE_TOKENS, dtype=jnp.int32)
    allowed = (segment[:, :, None] == segment[:, None, :]) & (
        row_index[:, None] >= row_index[None, :]
    )[None]
    local = jnp.arange(EXPERTS, dtype=jnp.int32)
    named = local % groups * local_experts + local // groups
    hits = jnp.any(routes[:, :, None] == named[None, None, :], axis=1)
    all_rows = jnp.arange(ROWS, dtype=jnp.int32)
    below = (all_rows[:, None] > all_rows[None, :]).astype(BF16)
    rank = mm("ts,se->te", below, hits.astype(BF16)).astype(jnp.int32)
    rank = jnp.where(hits, rank, -1)
    slot_id = jnp.arange(SLOTS, dtype=jnp.int32)
    place = rank.T[:, None, :] == slot_id[None, :, None]
    place_rows = place.astype(BF16).reshape(EXPERTS * SLOTS, ROWS)
    scale_one = rms_scale(plain_in)
    plain_one = plain_in * scale_one
    attention_input = (plain_one * gain_one[None, :]).astype(BF16)
    qkv = mm("td,de->te", attention_input, qkv_full)
    query = (
        rotary_apply(qkv[:, :Q_COLS].reshape(ROWS, QUERY_HEADS, HEAD_SIZE), cosine, sine)
        .astype(BF16)
        .reshape(MB, DEVICE_TOKENS, KEY_VALUE_HEADS, heads, HEAD_SIZE)
    )
    key = (
        rotary_apply(
            qkv[:, Q_COLS : Q_COLS + KV_COLS].reshape(ROWS, KEY_VALUE_HEADS, HEAD_SIZE),
            cosine,
            sine,
        )
        .astype(BF16)
        .reshape(MB, DEVICE_TOKENS, KEY_VALUE_HEADS, HEAD_SIZE)
    )
    value = (
        qkv[:, Q_COLS + KV_COLS :]
        .astype(BF16)
        .reshape(MB, DEVICE_TOKENS, KEY_VALUE_HEADS, HEAD_SIZE)
    )
    scores = mm("bqgrd,bkgd->bgrqk", query, key) * SCALE
    scores = jnp.where(allowed[:, None, None], scores, -1e30)
    exp_scores = jnp.exp(scores - jnp.max(scores, axis=-1, keepdims=True))
    probs = exp_scores / jnp.sum(exp_scores, axis=-1, keepdims=True)
    probs_low = probs.astype(BF16)
    mixed = mm("bgrqk,bkgd->bqgrd", probs_low, value).reshape(ROWS, Q_COLS).astype(BF16)
    middle = plain_in + mm("te,ed->td", mixed, o_full)
    scale_two = rms_scale(middle)
    plain_two = middle * scale_two
    ffn_in = (plain_two * gain_two[None, :]).astype(BF16)
    dispatch = mm("st,td->sd", place_rows, ffn_in).astype(BF16)
    received = exchange(
        dispatch.reshape(EXPERTS, SLOTS, MODEL_WIDTH), local_experts, inner
    ).reshape(EXPERTS * SLOTS, MODEL_WIDTH)
    logits = mm("td,de->te", ffn_in, r_full)
    logits = logits.reshape(ROWS, groups, local_experts).swapaxes(1, 2).reshape(ROWS, EXPERTS)
    logits = jnp.where(hits, logits, -jnp.inf)
    exp_logits = jnp.exp(logits - jnp.max(logits, axis=1, keepdims=True))
    gates = exp_logits / jnp.sum(exp_logits, axis=1, keepdims=True)
    slot_gates = jnp.sum(jnp.where(place, gates.T[:, None, :], 0.0), axis=2)
    cot_rows = mm("st,td->sd", place_rows, cotangent).reshape(EXPERTS, SLOTS, MODEL_WIDTH)
    grad_recv = exchange(
        (slot_gates[:, :, None] * cot_rows).astype(BF16), local_experts, inner
    ).reshape(EXPERTS * SLOTS, MODEL_WIDTH)
    gate_act = mm("sd,dh->sh", received, gate_full)
    up_act = mm("sd,dh->sh", received, up_full)
    sigmoid_g = jax.nn.sigmoid(gate_act)
    silu_gate = gate_act * sigmoid_g
    hidden = (silu_gate * up_act).astype(BF16)
    produced = mm("sh,hd->sd", hidden, down_full).astype(BF16)
    returned = exchange(
        produced.reshape(EXPERTS, SLOTS, MODEL_WIDTH), local_experts, inner
    ).reshape(EXPERTS * SLOTS, MODEL_WIDTH)
    grad_hidden = mm("sd,hd->sh", grad_recv, down_full)
    grad_gact = (grad_hidden * up_act * sigmoid_g * (1.0 + gate_act * (1.0 - sigmoid_g))).astype(
        BF16
    )
    grad_uact = (grad_hidden * silu_gate).astype(BF16)
    grad_inputs = (
        mm("sh,dh->sd", grad_gact, gate_full) + mm("sh,dh->sd", grad_uact, up_full)
    ).astype(BF16)
    grad_back = exchange(
        grad_inputs.reshape(EXPERTS, SLOTS, MODEL_WIDTH), local_experts, inner
    ).reshape(EXPERTS * SLOTS, MODEL_WIDTH)
    grad_down = grad_to_owners(mm("sh,sd->hd", hidden, grad_recv), inner, cross)
    grad_gate = grad_to_owners(mm("sd,sh->dh", received, grad_gact), inner, cross)
    grad_up = grad_to_owners(mm("sd,sh->dh", received, grad_uact), inner, cross)
    slot_column = slot_gates.reshape(EXPERTS * SLOTS, 1)
    part_one = slot_column.astype(BF16)
    rest = slot_column - part_one.astype(F32)
    part_two = rest.astype(BF16)
    part_three = (rest - part_two.astype(F32)).astype(BF16)
    combined = (
        mm("st,sd->td", place_rows * part_three, returned)
        + mm("st,sd->td", place_rows * part_two, returned)
        + mm("st,sd->td", place_rows * part_one, returned)
    )
    layer_out = (middle + combined).astype(BF16)
    products = mm("sd,td->st", returned, cotangent).reshape(EXPERTS, SLOTS, ROWS)
    grad_gates = jnp.sum(jnp.where(place, products, 0.0), axis=1).T
    grad_logits = gates * (grad_gates - jnp.sum(gates * grad_gates, axis=1, keepdims=True))
    grad_logits = (
        grad_logits.reshape(ROWS, local_experts, groups).swapaxes(1, 2).reshape(ROWS, EXPERTS)
    )
    grad_router = jnp.dot(ffn_in.astype(F32).T, grad_logits, precision=HIGH)
    grad_ffn_in = jnp.dot(grad_logits, r_full.astype(F32).T, precision=HIGH)
    grad_ffn_in = grad_ffn_in + mm("st,sd->td", place_rows, grad_back)
    grad_middle, grad_gain_two = norm_back(grad_ffn_in, gain_two, plain_two, scale_two)
    grad_middle = grad_middle + grad_out
    grad_attn = grad_middle.astype(BF16)
    grad_o = sum_to_owners(mm("te,td->ed", mixed, grad_attn).astype(BF16))
    grad_mix = (
        mm("td,ed->te", grad_attn, o_full)
        .astype(BF16)
        .reshape(MB, DEVICE_TOKENS, KEY_VALUE_HEADS, heads, HEAD_SIZE)
    )
    grad_value = mm("bgrqk,bqgrd->bkgd", probs_low, grad_mix).astype(BF16).reshape(ROWS, KV_COLS)
    grad_probs = mm("bqgrd,bkgd->bgrqk", grad_mix, value)
    row_inner = jnp.sum(probs * grad_probs, axis=-1, keepdims=True)
    grad_scores = (probs * (grad_probs - row_inner)).astype(BF16)
    grad_query = mm("bgrqk,bkgd->bqgrd", grad_scores, key) * SCALE
    grad_query = (
        rotary_apply(grad_query.reshape(ROWS, QUERY_HEADS, HEAD_SIZE), cosine, -sine)
        .astype(BF16)
        .reshape(ROWS, Q_COLS)
    )
    grad_key = mm("bgrqk,bqgrd->bkgd", grad_scores, query) * SCALE
    grad_key = (
        rotary_apply(grad_key.reshape(ROWS, KEY_VALUE_HEADS, HEAD_SIZE), cosine, -sine)
        .astype(BF16)
        .reshape(ROWS, KV_COLS)
    )
    grad_qkv = jnp.concatenate([grad_query, grad_key, grad_value], axis=1)
    grad_qkv_w = mm("td,te->de", attention_input, grad_qkv).astype(BF16)
    grad_attn_in = mm("te,de->td", grad_qkv, qkv_full)
    grad_plain, grad_gain_one = norm_back(grad_attn_in, gain_one, plain_one, scale_one)
    small_grads = jnp.concatenate(
        [
            grad_router,
            grad_gain_one[:, None],
            grad_gain_two[:, None],
            jnp.zeros((MODEL_WIDTH, SMALL_COLS // 2 - EXPERTS - 2), F32),
        ],
        axis=1,
    )
    small_high = small_grads.astype(BF16)
    small_low = (small_grads - small_high.astype(F32)).astype(BF16)
    owned = sum_to_owners(jnp.concatenate([grad_qkv_w, small_high, small_low], axis=1))
    small_owned = (
        owned[:, QKV_COLS : QKV_COLS + SMALL_COLS // 2] + owned[:, QKV_COLS + SMALL_COLS // 2 :]
    )
    grad_qkv_w = owned[:, :QKV_COLS]
    return (
        layer_out,
        grad_plain + grad_middle,
        grad_qkv_w[:, :Q_COLS],
        grad_qkv_w[:, Q_COLS : Q_COLS + KV_COLS],
        grad_qkv_w[:, Q_COLS + KV_COLS :],
        grad_o,
        small_owned[:, :EXPERTS],
        small_owned[:, EXPERTS],
        small_owned[:, EXPERTS + 1],
        grad_gate,
        grad_up,
        grad_down,
    )


def solution(mesh):
    in_specs = (
        P(("fsdp", "expert"), None),
        P(("fsdp", "expert"), None),
        P(("fsdp", "expert"), None),
        P(("fsdp", "expert"), None),
        P(("fsdp", "expert"), None),
        P(("fsdp", "expert"), None),
        P(("fsdp", "expert")),
        P(("fsdp", "expert")),
        P("expert", "fsdp", None),
        P("expert", "fsdp", None),
        P("expert", "fsdp", None),
        P(("fsdp", "expert"), None, None),
        P(("fsdp", "expert"), None),
        P(("fsdp", "expert"), None),
    )
    out_specs = (
        P(("fsdp", "expert"), None),
        P(("fsdp", "expert"), None),
        P(("fsdp", "expert"), None),
        P(("fsdp", "expert"), None),
        P(("fsdp", "expert"), None),
        P(("fsdp", "expert"), None),
        P(("fsdp", "expert"), None),
        P(("fsdp", "expert")),
        P(("fsdp", "expert")),
        P("expert", "fsdp", None),
        P("expert", "fsdp", None),
        P("expert", "fsdp", None),
    )
    return jax.shard_map(
        per_device, mesh=mesh, in_specs=in_specs, out_specs=out_specs, check_vma=False
    )
```

profile of v0, /device:TPU:0, one launch (start us, length us, event | category | flops | bytes accessed | tf_op | source)
XLA Modules:
  0.0 914.2 jit_solution(18132010783329984123)
XLA Ops:
  10.5 7.4 all-to-all-start.1
  19.5 25.6 %all-to-all-done.1 = bf16[16,64,512]{2,1,0:T(8,128)(2,1)S(1)} async-done(((bf16[16,64,512]{2,1,0:T(8,128)(2,1)}), bf16[16,64,512]{2,1,0:T(8,128)(2,1)S(1)}, u32[]{:S(2)}, u32[]{:S(2)}) %all-to-all-start.1) | async-done | bytes 1048608 | tf_op jit(solution)/shard_map/all_to_all | solution.py:90
  45.1 6.8 all-to-all-start.2
  52.9 49.8 %all-gather.2.cloned.1.call-done = bf16[1024,3200]{1,0:T(8,128)(2,1)} async-done(((bf16[32,3200]{1,0:T(8,128)(2,1)}), bf16[1024,3200]{1,0:T(8,128)(2,1)}) %all-gather.2.cloned.1.call-update) | async-done | bytes 6553616 | tf_op jit(solution)/shard_map/all_gather | solution.py:164
  126.8 11.0 %all-to-all-done.3 = bf16[16,32,1024]{2,1,0:T(8,128)(2,1)} async-done(((bf16[16,32,1024]{2,1,0:T(8,128)(2,1)}), bf16[16,32,1024]{2,1,0:T(8,128)(2,1)}, u32[]{:S(2)}, u32[]{:S(2)}) %all-to-all-start.3) | async-done | bytes 1048608 | tf_op jit(solution)/shard_map/all_to_all | solution.py:90
  149.6 110.8 %all-to-all-done = bf16[32,80,1024]{2,1,0:T(8,128)(2,1)} async-done(((bf16[32,80,1024]{2,1,0:T(8,128)(2,1)}), bf16[32,80,1024]{2,1,0:T(8,128)(2,1)}, u32[]{:S(2)}, u32[]{:S(2)}) %all-to-all-start) | async-done | bytes 5242912 | tf_op jit(solution)/shard_map/all_to_all | solution.py:115
  265.3 8.1 fusion.120
  273.4 7.1 fusion.119
  280.6 100.8 %all-to-all-done.5 = bf16[32,80,1024]{2,1,0:T(8,128)(2,1)} async-done(((bf16[32,80,1024]{2,1,0:T(8,128)(2,1)}), bf16[32,80,1024]{2,1,0:T(8,128)(2,1)}, u32[]{:S(2)}, u32[]{:S(2)}) %all-to-all-start.5) | async-done | bytes 5242912 | tf_op jit(solution)/shard_map/all_to_all | solution.py:115
  381.4 12.0 %multiply_convert_fusion.1 = (bf16[2560,512]{1,0:T(8,128)(2,1)}, bf16[2560,512]{1,0:T(8,128)(2,1)S(1)}, bf16[2560,512]{1,0:T(8,128)(2,1)}) fusion(f32[2560,512]{1,0:T(8,128)} %fusion.119, f32[2560,512]{1,0:T(8,128)} %fusion.120, bf16[2560,1024]{1,0:T(8,128)(2,1)} %bitcast.37, bf16[512,1024]{1,0:T(8,128)(2,1)} %bitcast.26), kind=kOutput, calls=%fused_computation.6 | convolution fusion | flops 2704015360 | bytes 24641536 | tf_op jit(solution)/shard_map/sd,hd->sh/dot_general | solution.py:30
  401.9 8.0 reduce.10
  425.3 8.0 reduce.11
  440.3 7.2 all-to-all-start.10
  447.5 7.2 convolution_convert_fusion.1
  454.8 15.6 %all-to-all-done.10 = bf16[16,2,16384]{2,1,0:T(2,128)(2,1)S(1)} async-done(((bf16[16,2,16384]{2,1,0:T(2,128)(2,1)}), bf16[16,2,16384]{2,1,0:T(2,128)(2,1)S(1)}, u32[]{:S(2)}, u32[]{:S(2)}) %all-to-all-start.10) | async-done | bytes 1048608 | tf_op jit(solution)/shard_map/all_to_all | solution.py:103
  471.4 6.9 all-to-all-start.4
  489.4 105.0 %all-to-all-done.4 = bf16[32,80,1024]{2,1,0:T(8,128)(2,1)} async-done(((bf16[32,80,1024]{2,1,0:T(8,128)(2,1)}), bf16[32,80,1024]{2,1,0:T(8,128)(2,1)}, u32[]{:S(2)}, u32[]{:S(2)}) %all-to-all-start.4) | async-done | bytes 5242912 | tf_op jit(solution)/shard_map/all_to_all | solution.py:115
  607.7 7.8 reduce.12
  622.5 92.9 %all-to-all-done.6 = bf16[32,80,1024]{2,1,0:T(8,128)(2,1)} async-done(((bf16[32,80,1024]{2,1,0:T(8,128)(2,1)}), bf16[32,80,1024]{2,1,0:T(8,128)(2,1)}, u32[]{:S(2)}, u32[]{:S(2)}) %all-to-all-start.6) | async-done | bytes 5242912 | tf_op jit(solution)/shard_map/all_to_all | solution.py:115
  732.8 10.2 %all-to-all-done.11 = bf16[16,2,16384]{2,1,0:T(2,128)(2,1)S(1)} async-done(((bf16[16,2,16384]{2,1,0:T(2,128)(2,1)}), bf16[16,2,16384]{2,1,0:T(2,128)(2,1)S(1)}, u32[]{:S(2)}, u32[]{:S(2)}) %all-to-all-start.11) | async-done | bytes 1048608 | tf_op jit(solution)/shard_map/all_to_all | solution.py:103
  743.0 6.9 all-to-all-start.8
  783.1 7.7 concatenate.57
  790.8 7.7 all-to-all-done.8
  842.4 59.5 %all-to-all-done.7 = bf16[32,32,2176]{2,1,0:T(8,128)(2,1)} async-done(((bf16[32,32,2176]{2,1,0:T(8,128)(2,1)}), bf16[32,32,2176]{2,1,0:T(8,128)(2,1)}, u32[]{:S(2)}, u32[]{:S(2)}) %all-to-all-start.7) | async-done | bytes 4456480 | tf_op jit(solution)/shard_map/all_to_all | solution.py:128
  (228 shorter events, 208.4 us)
Async XLA Ops:
  7.2 10.8 %copy-start.41 = (s32[1,2,4]{2,1,0:T(2,128)S(1)}, s32[1,2,4]{2,1,0:T(2,128)}, u32[]{:S(2)}) copy-start(s32[1,2,4]{2,1,0:T(2,128)} %param.25) | copy-start | bytes 100
  7.2 11.2 %copy-start.40 = (s32[256,8]{0,1:T(8,128)S(1)}, s32[256,8]{0,1:T(8,128)}, u32[]{:S(2)}) copy-start(s32[256,8]{0,1:T(8,128)} %param.26) | copy-start | bytes 24580
  7.2 12.1 %copy-start.11 = (bf16[256,1024]{1,0:T(8,128)(2,1)S(1)}, bf16[256,1024]{1,0:T(8,128)(2,1)}, u32[]{:S(2)}) copy-start(bf16[256,1024]{1,0:T(8,128)(2,1)} %param.14) | copy-start | bytes 1572868
  7.2 95.5 %all-gather.2.cloned.1.call-start = ((), (), s32[]{:S(2)}) async-start(), calls=%async_computation.12 | async-start | bytes 6758400 | tf_op jit(solution)/shard_map/all_gather | solution.py:164
  10.5 34.6 %all-to-all-start.1 = ((bf16[16,64,512]{2,1,0:T(8,128)(2,1)}), bf16[16,64,512]{2,1,0:T(8,128)(2,1)S(1)}, u32[]{:S(2)}, u32[]{:S(2)}) async-start(bf16[16,64,512]{2,1,0:T(8,128)(2,1)} %param.22), calls=%async_computation.1 | async-start | bytes 2097152 | tf_op jit(solution)/shard_map/all_to_all | solution.py:90
  45.1 62.6 %copy-start.17 = (bf16[16,64,512]{2,1,0:T(8,128)(2,1)}, bf16[16,64,512]{2,1,0:T(8,128)(2,1)S(1)}, u32[]{:S(2)}) copy-start(bf16[16,64,512]{2,1,0:T(8,128)(2,1)S(1)} %all-to-all-done.1) | copy-start | bytes 3145732
  45.1 65.4 %all-to-all-start.2 = ((bf16[16,64,512]{2,1,0:T(8,128)(2,1)}), bf16[16,64,512]{2,1,0:T(8,128)(2,1)}, u32[]{:S(2)}, u32[]{:S(2)}) async-start(bf16[16,64,512]{2,1,0:T(8,128)(2,1)} %param.23), calls=%async_computation.2 | async-start | bytes 2097152 | tf_op jit(solution)/shard_map/all_to_all | solution.py:90
  52.0 55.7 %copy-start.42 = (f32[256]{0:T(256)}, f32[256]{0:T(256)S(1)}, u32[]{:S(2)}) copy-start(f32[256]{0:T(256)S(1)} %add_rsqrt_fusion.1) | copy-start | bytes 3076
  104.2 18.6 %copy-start.31 = (f32[1024]{0:T(1024)}, f32[1024]{0:T(1024)S(1)}, u32[]{:S(2)}) copy-start(f32[1024]{0:T(1024)S(1)} %get-tuple-element.12) | copy-start | bytes 12292
  110.5 27.3 %all-to-all-start.3 = ((bf16[16,32,1024]{2,1,0:T(8,128)(2,1)}), bf16[16,32,1024]{2,1,0:T(8,128)(2,1)}, u32[]{:S(2)}, u32[]{:S(2)}) async-start(bf16[16,32,1024]{2,1,0:T(8,128)(2,1)} %param.24), calls=%async_computation.3 | async-start | bytes 2097152 | tf_op jit(solution)/shard_map/all_to_all | solution.py:90
  122.9 21.3 %copy-start = (bf16[256,1024]{1,0:T(8,128)(2,1)}, bf16[256,1024]{1,0:T(8,128)(2,1)S(1)}, u32[]{:S(2)}) copy-start(bf16[256,1024]{1,0:T(8,128)(2,1)S(1)} %multiply_convert_fusion.4) | copy-start | bytes 1572868
  137.8 8.6 copy-start.24
  137.8 122.6 %all-to-all-start = ((bf16[32,80,1024]{2,1,0:T(8,128)(2,1)}), bf16[32,80,1024]{2,1,0:T(8,128)(2,1)}, u32[]{:S(2)}, u32[]{:S(2)}) async-start(bf16[32,80,1024]{2,1,0:T(8,128)(2,1)} %bitcast.235), calls=%async_computation | async-start | bytes 10485760 | tf_op jit(solution)/shard_map/all_to_all | solution.py:115
  260.4 121.0 %all-to-all-start.5 = ((bf16[32,80,1024]{2,1,0:T(8,128)(2,1)}), bf16[32,80,1024]{2,1,0:T(8,128)(2,1)}, u32[]{:S(2)}, u32[]{:S(2)}) async-start(bf16[32,80,1024]{2,1,0:T(8,128)(2,1)} %multiply_convert_fusion), calls=%async_computation.5 | async-start | bytes 10485760 | tf_op jit(solution)/shard_map/all_to_all | solution.py:115
  265.3 8.1 copy-start.18
  412.5 27.8 %all-to-all-start.9 = ((bf16[16,2,16384]{2,1,0:T(2,128)(2,1)}), bf16[16,2,16384]{2,1,0:T(2,128)(2,1)}, u32[]{:S(2)}, u32[]{:S(2)}) async-start(bf16[16,2,16384]{2,1,0:T(2,128)(2,1)} %reshape.483), calls=%async_computation.9 | async-start | bytes 2097152 | tf_op jit(solution)/shard_map/all_to_all | solution.py:103
  440.3 30.1 %all-to-all-start.10 = ((bf16[16,2,16384]{2,1,0:T(2,128)(2,1)}), bf16[16,2,16384]{2,1,0:T(2,128)(2,1)S(1)}, u32[]{:S(2)}, u32[]{:S(2)}) async-start(bf16[16,2,16384]{2,1,0:T(2,128)(2,1)} %reshape.485), calls=%async_computation.10 | async-start | bytes 2097152 | tf_op jit(solution)/shard_map/all_to_all | solution.py:103
  471.4 123.0 %all-to-all-start.4 = ((bf16[32,80,1024]{2,1,0:T(8,128)(2,1)}), bf16[32,80,1024]{2,1,0:T(8,128)(2,1)}, u32[]{:S(2)}, u32[]{:S(2)}) async-start(bf16[32,80,1024]{2,1,0:T(8,128)(2,1)} %bitcast.245), calls=%async_computation.4 | async-start | bytes 10485760 | tf_op jit(solution)/shard_map/all_to_all | solution.py:115
  594.4 121.0 %all-to-all-start.6 = ((bf16[32,80,1024]{2,1,0:T(8,128)(2,1)}), bf16[32,80,1024]{2,1,0:T(8,128)(2,1)}, u32[]{:S(2)}, u32[]{:S(2)}) async-start(bf16[32,80,1024]{2,1,0:T(8,128)(2,1)} %bitcast.244), calls=%async_computation.6 | async-start | bytes 10485760 | tf_op jit(solution)/shard_map/all_to_all | solution.py:115
  715.5 27.5 %all-to-all-start.11 = ((bf16[16,2,16384]{2,1,0:T(2,128)(2,1)}), bf16[16,2,16384]{2,1,0:T(2,128)(2,1)S(1)}, u32[]{:S(2)}, u32[]{:S(2)}) async-start(bf16[16,2,16384]{2,1,0:T(2,128)(2,1)} %reshape.487), calls=%async_computation.11 | async-start | bytes 2097152 | tf_op jit(solution)/shard_map/all_to_all | solution.py:103
  743.0 10.1 %copy-start.4 = (bf16[16,2,16384]{2,1,0:T(2,128)(2,1)}, bf16[16,2,16384]{2,1,0:T(2,128)(2,1)S(1)}, u32[]{:S(2)}) copy-start(bf16[16,2,16384]{2,1,0:T(2,128)(2,1)S(1)} %all-to-all-done.11) | copy-start | bytes 3145732
  743.0 55.6 %all-to-all-start.8 = ((bf16[32,32,1024]{2,1,0:T(8,128)(2,1)}), bf16[32,32,1024]{2,1,0:T(8,128)(2,1)}, u32[]{:S(2)}, u32[]{:S(2)}) async-start(bf16[32,32,1024]{2,1,0:T(8,128)(2,1)} %bitcast.237), calls=%async_computation.8 | async-start | bytes 4194304 | tf_op jit(solution)/shard_map/all_to_all | solution.py:128
  749.9 9.1 copy-start.34
  798.6 103.3 %all-to-all-start.7 = ((bf16[32,32,2176]{2,1,0:T(8,128)(2,1)}), bf16[32,32,2176]{2,1,0:T(8,128)(2,1)}, u32[]{:S(2)}, u32[]{:S(2)}) async-start(bf16[32,32,2176]{2,1,0:T(8,128)(2,1)} %bitcast.236), calls=%async_computation.7 | async-start | bytes 8912896 | tf_op jit(solution)/shard_map/all_to_all | solution.py:128
  (36 other events, 117.9 us)
Sparse Core Ops, SparseCore 0:
  11.5 91.1 all-gather.1
where the time goes:
time: 924 us; the launch traced here: 914 us
  waiting for transfers between devices  593 us (64%)
  matrix products  126 us (14%)
  local copies, waits for them, and re-layouts  70.4 us (8%)
  starting transfers between devices  69.6 us (8%)
  other arithmetic  39.4 us (4%)
  between operations  15.5 us (2%)
    all_to_all x4, waiting for transfers between devices, exchange(): return lax.all_to_all(rows, BOTH, split_axis=0, concat_axis=0, tiled=True)  410 us
    dot_general x29, matrix products, mm(): return jnp.einsum(spec, a, b, preferred_element_type=F32)  120 us
    all_to_all x2, waiting for transfers between devices, sum_to_owners(): parts = lax.all_to_all(parts, BOTH, split_axis=0, concat_axis=0, tiled=True)  67.2 us
    all_gather x1, waiting for transfers between devices, per_device(): full = lax.all_gather(packed, BOTH, axis=0, tiled=True)  49.8 us
    all_to_all x3, waiting for transfers between devices, weight_to_expert(): lax.all_to_all(weight, 'fsdp', split_axis=0, concat_axis=1, axis_index_gr...  36.6 us
    unnamed x106, local copies, waits for them, and re-layouts  35.7 us
    all_to_all x3, waiting for transfers between devices, grad_to_owners(): lax.all_to_all(grad.astype(BF16)[None], 'fsdp', split_axis=1, concat_axis...  30.2 us
    unnamed x4, other arithmetic  23.9 us
  transfers between devices with their start and end apart: 13, of which 12 were waited for; matrix products, arithmetic and copies ran while one was open for 21% of the time, Pallas kernels for 0%

commit v1 on v0

--- a/solution.py
+++ b/solution.py
@@ -1,7 +1,9 @@
+import functools
 import jax
 import jax.numpy as jnp
 from jax import lax
 from jax.sharding import PartitionSpec as P
+from jax.lax import axis_index, axis_size, ppermute
 
 MODEL_WIDTH = 1024
 QUERY_HEADS = 16
@@ -24,6 +26,23 @@
 BOTH = ("fsdp", "expert")
 F32 = jnp.float32
 BF16 = jnp.bfloat16
+
+
+def goods_produce(my_data, mesh_name):
+    next_value = axis_size(mesh_name)
+    val2, opened = (next_value, axis_index(mesh_name))
+    all_values, frame_out = (my_data, 1)
+    while frame_out < val2:
+        moved = tuple(((num, num ^ frame_out) for num in range(val2)))
+        ready = ppermute(all_values, axis_name=mesh_name, perm=moved)
+        q_next = jnp.concatenate([all_values, ready], 0)
+        met_up = jnp.concatenate([ready, all_values], 0)
+        all_values = jnp.where(opened & frame_out == 0, q_next, met_up)
+        frame_out = 2 * frame_out
+    return all_values
+
+
+_carry_pipes = functools.partial(goods_produce, mesh_name=BOTH)
 
 
 def mm(spec, a, b):
@@ -161,7 +180,7 @@
     packed = jnp.concatenate(
         [query_weight, key_projection, value_projection, output_weight, small], axis=1
     )
-    full = lax.all_gather(packed, BOTH, axis=0, tiled=True)
+    full = _carry_pipes(packed)
     qkv_full = full[:, :QKV_COLS]
     o_full = full[:, QKV_COLS : QKV_COLS + MODEL_WIDTH]
     small_full = full[:, QKV_COLS + MODEL_WIDTH :]

time: 924 us -> 1080 us (1.17)
  waiting for transfers between devices: 593 us -> 742 us
  between operations: 15.5 us -> 1.9 us
  starting transfers between devices: 69.6 us -> 82.4 us
    all_to_all x3, waiting for transfers between devices: 36.6 us -> 174 us  [weight_to_expert(): lax.all_to_all(weight, 'fsdp', split_axis=0, concat_axis=1, axis_index_gr...]
    ppermute x0 -> x5, waiting for transfers between devices: none -> 60.7 us  [goods_produce(): ready = ppermute(all_values, axis_name=mesh_name, perm=moved)]
    all_gather x1 -> x0, waiting for transfers between devices: 49.8 us -> none  [per_device(): full = lax.all_gather(packed, BOTH, axis=0, tiled=True)]
    unnamed x106 -> x104, local copies, waits for them, and re-layouts: 35.7 us -> 29.9 us
  transfers between devices with their start and end apart: 13 -> 17, of which waited for: 12 -> 16; matrix products, arithmetic and copies ran while one was open for 21% -> 18% of each run, Pallas kernels for 0% -> 0%
where the time goes in v1:
time: 1080 us; the launch traced here: 1070 us
  waiting for transfers between devices  742 us (69%)
  matrix products  126 us (12%)
  starting transfers between devices  82.4 us (8%)
  local copies, waits for them, and re-layouts  67.3 us (6%)
  other arithmetic  49.3 us (5%)
    all_to_all x4, waiting for transfers between devices, exchange(): return lax.all_to_all(rows, BOTH, split_axis=0, concat_axis=0, tiled=True)  408 us
    all_to_all x3, waiting for transfers between devices, weight_to_expert(): lax.all_to_all(weight, 'fsdp', split_axis=0, concat_axis=1, axis_index_gr...  174 us
    dot_general x29, matrix products, mm(): return jnp.einsum(spec, a, b, preferred_element_type=F32)  121 us
    all_to_all x2, waiting for transfers between devices, sum_to_owners(): parts = lax.all_to_all(parts, BOTH, split_axis=0, concat_axis=0, tiled=True)  69.3 us
    ppermute x5, waiting for transfers between devices, goods_produce(): ready = ppermute(all_values, axis_name=mesh_name, perm=moved)  60.7 us
    unnamed x104, local copies, waits for them, and re-layouts  29.9 us
    all_to_all x3, waiting for transfers between devices, grad_to_owners(): lax.all_to_all(grad.astype(BF16)[None], 'fsdp', split_axis=1, concat_axis...  29.9 us
    unnamed x4, other arithmetic  24.2 us
  transfers between devices with their start and end apart: 17, of which 16 were waited for; matrix products, arithmetic and copies ran while one was open for 18% of the time, Pallas kernels for 0%

profile of v1, /device:TPU:0, one launch (start us, length us, event | category | flops | bytes accessed | tf_op | source)
XLA Modules:
  0.0 1068.8 jit_solution(798814477755803466)
XLA Ops:
  15.1 18.5 %collective-permute-done.2 = bf16[128,3200]{1,0:T(8,128)(2,1)S(1)} collective-permute-done((bf16[128,3200]{1,0:T(8,128)(2,1)S(1)}, bf16[128,3200]{1,0:T(8,128)(2,1)S(1)}, u32[]{:S(2)}, u32[]{:S(2)}) %collective-permute-start.2) | collective-permute-done | bytes 819232 | tf_op jit(solution)/shard_map/ppermute | solution.py:37
  35.9 35.3 %collective-permute-done.3 = bf16[256,3200]{1,0:T(8,128)(2,1)} collective-permute-done((bf16[256,3200]{1,0:T(8,128)(2,1)S(1)}, bf16[256,3200]{1,0:T(8,128)(2,1)}, u32[]{:S(2)}, u32[]{:S(2)}) %collective-permute-start.3) | collective-permute-done | bytes 1638432 | tf_op jit(solution)/shard_map/ppermute | solution.py:37
  85.7 149.9 %all-to-all-done.1 = bf16[16,64,512]{2,1,0:T(8,128)(2,1)} async-done(((bf16[16,64,512]{2,1,0:T(8,128)(2,1)}), bf16[16,64,512]{2,1,0:T(8,128)(2,1)}, u32[]{:S(2)}, u32[]{:S(2)}) %all-to-all-start.1) | async-done | bytes 1048608 | tf_op jit(solution)/shard_map/all_to_all | solution.py:109
  235.5 10.1 all-to-all-start.2
  257.1 11.5 %all-to-all-done.2 = bf16[16,64,512]{2,1,0:T(8,128)(2,1)} async-done(((bf16[16,64,512]{2,1,0:T(8,128)(2,1)}), bf16[16,64,512]{2,1,0:T(8,128)(2,1)}, u32[]{:S(2)}, u32[]{:S(2)}) %all-to-all-start.2) | async-done | bytes 1048608 | tf_op jit(solution)/shard_map/all_to_all | solution.py:109
  285.7 12.6 %all-to-all-done.3 = bf16[16,32,1024]{2,1,0:T(8,128)(2,1)} async-done(((bf16[16,32,1024]{2,1,0:T(8,128)(2,1)}), bf16[16,32,1024]{2,1,0:T(8,128)(2,1)}, u32[]{:S(2)}, u32[]{:S(2)}) %all-to-all-start.3) | async-done | bytes 1048608 | tf_op jit(solution)/shard_map/all_to_all | solution.py:109
  298.3 7.0 all-to-all-start
  310.7 110.7 %all-to-all-done = bf16[32,80,1024]{2,1,0:T(8,128)(2,1)} async-done(((bf16[32,80,1024]{2,1,0:T(8,128)(2,1)}), bf16[32,80,1024]{2,1,0:T(8,128)(2,1)}, u32[]{:S(2)}, u32[]{:S(2)}) %all-to-all-start) | async-done | bytes 5242912 | tf_op jit(solution)/shard_map/all_to_all | solution.py:134
  426.2 8.0 fusion.120
  434.2 8.0 fusion.119
  442.2 100.1 %all-to-all-done.5 = bf16[32,80,1024]{2,1,0:T(8,128)(2,1)} async-done(((bf16[32,80,1024]{2,1,0:T(8,128)(2,1)}), bf16[32,80,1024]{2,1,0:T(8,128)(2,1)}, u32[]{:S(2)}, u32[]{:S(2)}) %all-to-all-start.5) | async-done | bytes 5242912 | tf_op jit(solution)/shard_map/all_to_all | solution.py:134
  542.3 12.2 %multiply_convert_fusion.1 = (bf16[2560,512]{1,0:T(8,128)(2,1)}, bf16[2560,512]{1,0:T(8,128)(2,1)S(1)}, bf16[2560,512]{1,0:T(8,128)(2,1)}) fusion(f32[2560,512]{1,0:T(8,128)} %fusion.119, f32[2560,512]{1,0:T(8,128)} %fusion.120, bf16[2560,1024]{1,0:T(8,128)(2,1)} %bitcast.37, bf16[512,1024]{1,0:T(8,128)(2,1)} %bitcast.26), kind=kOutput, calls=%fused_computation.7 | convolution fusion | flops 2704015360 | bytes 24641536 | tf_op jit(solution)/shard_map/sd,hd->sh/dot_general | solution.py:49
  564.3 8.0 reduce.10
  588.1 8.0 reduce.11
  601.9 7.0 all-to-all-start.10
  608.8 7.2 convolution_convert_fusion.1
  616.1 15.6 %all-to-all-done.10 = bf16[16,2,16384]{2,1,0:T(2,128)(2,1)S(1)} async-done(((bf16[16,2,16384]{2,1,0:T(2,128)(2,1)}), bf16[16,2,16384]{2,1,0:T(2,128)(2,1)S(1)}, u32[]{:S(2)}, u32[]{:S(2)}) %all-to-all-start.10) | async-done | bytes 1048608 | tf_op jit(solution)/shard_map/all_to_all | solution.py:122
  650.9 104.8 %all-to-all-done.4 = bf16[32,80,1024]{2,1,0:T(8,128)(2,1)} async-done(((bf16[32,80,1024]{2,1,0:T(8,128)(2,1)}), bf16[32,80,1024]{2,1,0:T(8,128)(2,1)}, u32[]{:S(2)}, u32[]{:S(2)}) %all-to-all-start.4) | async-done | bytes 5242912 | tf_op jit(solution)/shard_map/all_to_all | solution.py:134
  770.4 8.1 reduce.12
  784.2 92.5 %all-to-all-done.6 = bf16[32,80,1024]{2,1,0:T(8,128)(2,1)} async-done(((bf16[32,80,1024]{2,1,0:T(8,128)(2,1)}), bf16[32,80,1024]{2,1,0:T(8,128)(2,1)}, u32[]{:S(2)}, u32[]{:S(2)}) %all-to-all-start.6) | async-done | bytes 5242912 | tf_op jit(solution)/shard_map/all_to_all | solution.py:134
  894.6 10.1 all-to-all-done.11
  945.0 7.8 concatenate.97
  952.7 7.5 all-to-all-done.8
  1001.7 61.8 %all-to-all-done.7 = bf16[32,32,2176]{2,1,0:T(8,128)(2,1)} async-done(((bf16[32,32,2176]{2,1,0:T(8,128)(2,1)}), bf16[32,32,2176]{2,1,0:T(8,128)(2,1)}, u32[]{:S(2)}, u32[]{:S(2)}) %all-to-all-start.7) | async-done | bytes 4456480 | tf_op jit(solution)/shard_map/all_to_all | solution.py:147
  (238 shorter events, 244.4 us)
Async XLA Ops:
  3.1 8.1 collective-permute-start
  11.3 1.8 collective-permute-start.1
  13.3 20.4 %collective-permute-start.2 = (bf16[128,3200]{1,0:T(8,128)(2,1)S(1)}, bf16[128,3200]{1,0:T(8,128)(2,1)S(1)}, u32[]{:S(2)}, u32[]{:S(2)}) collective-permute-start(bf16[128,3200]{1,0:T(8,128)(2,1)S(1)} %maximum_select_fusion.3), channel_id=1, source_target_pairs={{0,4},{1,5},{2,6},{3,7},{4,0},{5,1},{6,2},{7,3},{8,12},{9,13},{10,... | collective-permute-start | bytes 2457608 | tf_op jit(solution)/shard_map/ppermute | solution.py:37
  34.0 37.2 %collective-permute-start.3 = (bf16[256,3200]{1,0:T(8,128)(2,1)S(1)}, bf16[256,3200]{1,0:T(8,128)(2,1)}, u32[]{:S(2)}, u32[]{:S(2)}) collective-permute-start(bf16[256,3200]{1,0:T(8,128)(2,1)S(1)} %maximum_select_fusion.2), channel_id=1, source_target_pairs={{0,8},{1,9},{2,10},{3,11},{4,12},{5,13},{6,14},{7,15},{8,0},{9,1},... | collective-permute-start | bytes 4915208 | tf_op jit(solution)/shard_map/ppermute | solution.py:37
  35.8 46.0 %copy-start.39 = (s32[256,8]{0,1:T(8,128)S(1)}, s32[256,8]{0,1:T(8,128)}, u32[]{:S(2)}) copy-start(s32[256,8]{0,1:T(8,128)} %param.26) | copy-start | bytes 24580
  35.8 46.2 %copy-start.40 = (s32[1,2,4]{2,1,0:T(2,128)S(1)}, s32[1,2,4]{2,1,0:T(2,128)}, u32[]{:S(2)}) copy-start(s32[1,2,4]{2,1,0:T(2,128)} %param.25) | copy-start | bytes 100
  74.7 170.9 %collective-permute-start.4 = (bf16[512,3200]{1,0:T(8,128)(2,1)S(1)}, bf16[512,3200]{1,0:T(8,128)(2,1)}, u32[]{:S(2)}, u32[]{:S(2)}) collective-permute-start(bf16[512,3200]{1,0:T(8,128)(2,1)S(1)} %maximum_select_fusion.1), channel_id=1, source_target_pairs={{0,16},{1,17},{2,18},{3,19},{4,20},{5,21},{6,22},{7,23},{8,24},{9,... | collective-permute-start | bytes 9830408 | tf_op jit(solution)/shard_map/ppermute | solution.py:37
  77.5 158.0 %all-to-all-start.1 = ((bf16[16,64,512]{2,1,0:T(8,128)(2,1)}), bf16[16,64,512]{2,1,0:T(8,128)(2,1)}, u32[]{:S(2)}, u32[]{:S(2)}) async-start(bf16[16,64,512]{2,1,0:T(8,128)(2,1)} %param.22), calls=%async_computation.1 | async-start | bytes 2097152 | tf_op jit(solution)/shard_map/all_to_all | solution.py:109
  85.3 165.9 %copy-start.41 = (f32[256]{0:T(256)}, f32[256]{0:T(256)S(1)}, u32[]{:S(2)}) copy-start(f32[256]{0:T(256)S(1)} %add_rsqrt_fusion.1) | copy-start | bytes 3076
  235.5 33.0 %all-to-all-start.2 = ((bf16[16,64,512]{2,1,0:T(8,128)(2,1)}), bf16[16,64,512]{2,1,0:T(8,128)(2,1)}, u32[]{:S(2)}, u32[]{:S(2)}) async-start(bf16[16,64,512]{2,1,0:T(8,128)(2,1)} %param.23), calls=%async_computation.2 | async-start | bytes 2097152 | tf_op jit(solution)/shard_map/all_to_all | solution.py:109
  268.5 29.8 %all-to-all-start.3 = ((bf16[16,32,1024]{2,1,0:T(8,128)(2,1)}), bf16[16,32,1024]{2,1,0:T(8,128)(2,1)}, u32[]{:S(2)}, u32[]{:S(2)}) async-start(bf16[16,32,1024]{2,1,0:T(8,128)(2,1)} %param.24), calls=%async_computation.3 | async-start | bytes 2097152 | tf_op jit(solution)/shard_map/all_to_all | solution.py:109
  281.9 23.4 %copy-start.1 = (bf16[256,1024]{1,0:T(8,128)(2,1)}, bf16[256,1024]{1,0:T(8,128)(2,1)S(1)}, u32[]{:S(2)}) copy-start(bf16[256,1024]{1,0:T(8,128)(2,1)S(1)} %multiply_convert_fusion.4) | copy-start | bytes 1572868
  298.3 123.1 %all-to-all-start = ((bf16[32,80,1024]{2,1,0:T(8,128)(2,1)}), bf16[32,80,1024]{2,1,0:T(8,128)(2,1)}, u32[]{:S(2)}, u32[]{:S(2)}) async-start(bf16[32,80,1024]{2,1,0:T(8,128)(2,1)} %bitcast.235), calls=%async_computation | async-start | bytes 10485760 | tf_op jit(solution)/shard_map/all_to_all | solution.py:134
  421.4 120.9 %all-to-all-start.5 = ((bf16[32,80,1024]{2,1,0:T(8,128)(2,1)}), bf16[32,80,1024]{2,1,0:T(8,128)(2,1)}, u32[]{:S(2)}, u32[]{:S(2)}) async-start(bf16[32,80,1024]{2,1,0:T(8,128)(2,1)} %multiply_convert_fusion), calls=%async_computation.5 | async-start | bytes 10485760 | tf_op jit(solution)/shard_map/all_to_all | solution.py:134
  573.9 27.9 %all-to-all-start.9 = ((bf16[16,2,16384]{2,1,0:T(2,128)(2,1)}), bf16[16,2,16384]{2,1,0:T(2,128)(2,1)S(1)}, u32[]{:S(2)}, u32[]{:S(2)}) async-start(bf16[16,2,16384]{2,1,0:T(2,128)(2,1)} %reshape.483), calls=%async_computation.9 | async-start | bytes 2097152 | tf_op jit(solution)/shard_map/all_to_all | solution.py:122
  601.9 14.2 %copy-start.4 = (bf16[16,2,16384]{2,1,0:T(2,128)(2,1)}, bf16[16,2,16384]{2,1,0:T(2,128)(2,1)S(1)}, u32[]{:S(2)}) copy-start(bf16[16,2,16384]{2,1,0:T(2,128)(2,1)S(1)} %all-to-all-done.9) | copy-start | bytes 3145732
  601.9 29.8 %all-to-all-start.10 = ((bf16[16,2,16384]{2,1,0:T(2,128)(2,1)}), bf16[16,2,16384]{2,1,0:T(2,128)(2,1)S(1)}, u32[]{:S(2)}, u32[]{:S(2)}) async-start(bf16[16,2,16384]{2,1,0:T(2,128)(2,1)} %reshape.485), calls=%async_computation.10 | async-start | bytes 2097152 | tf_op jit(solution)/shard_map/all_to_all | solution.py:122
  632.7 123.0 %all-to-all-start.4 = ((bf16[32,80,1024]{2,1,0:T(8,128)(2,1)}), bf16[32,80,1024]{2,1,0:T(8,128)(2,1)}, u32[]{:S(2)}, u32[]{:S(2)}) async-start(bf16[32,80,1024]{2,1,0:T(8,128)(2,1)} %bitcast.245), calls=%async_computation.4 | async-start | bytes 10485760 | tf_op jit(solution)/shard_map/all_to_all | solution.py:134
  755.7 121.1 %all-to-all-start.6 = ((bf16[32,80,1024]{2,1,0:T(8,128)(2,1)}), bf16[32,80,1024]{2,1,0:T(8,128)(2,1)}, u32[]{:S(2)}, u32[]{:S(2)}) async-start(bf16[32,80,1024]{2,1,0:T(8,128)(2,1)} %bitcast.244), calls=%async_computation.6 | async-start | bytes 10485760 | tf_op jit(solution)/shard_map/all_to_all | solution.py:134
  770.4 9.7 copy-start.24
  876.8 27.9 %all-to-all-start.11 = ((bf16[16,2,16384]{2,1,0:T(2,128)(2,1)}), bf16[16,2,16384]{2,1,0:T(2,128)(2,1)S(1)}, u32[]{:S(2)}, u32[]{:S(2)}) async-start(bf16[16,2,16384]{2,1,0:T(2,128)(2,1)} %reshape.487), calls=%async_computation.11 | async-start | bytes 2097152 | tf_op jit(solution)/shard_map/all_to_all | solution.py:122
  904.7 10.1 copy-start.8
  904.7 55.6 %all-to-all-start.8 = ((bf16[32,32,1024]{2,1,0:T(8,128)(2,1)}), bf16[32,32,1024]{2,1,0:T(8,128)(2,1)}, u32[]{:S(2)}, u32[]{:S(2)}) async-start(bf16[32,32,1024]{2,1,0:T(8,128)(2,1)} %bitcast.237), calls=%async_computation.8 | async-start | bytes 4194304 | tf_op jit(solution)/shard_map/all_to_all | solution.py:147
  960.3 103.2 %all-to-all-start.7 = ((bf16[32,32,2176]{2,1,0:T(8,128)(2,1)}), bf16[32,32,2176]{2,1,0:T(8,128)(2,1)}, u32[]{:S(2)}, u32[]{:S(2)}) async-start(bf16[32,32,2176]{2,1,0:T(8,128)(2,1)} %bitcast.236), calls=%async_computation.7 | async-start | bytes 8912896 | tf_op jit(solution)/shard_map/all_to_all | solution.py:147
  (39 other events, 145.3 us)
